TPU v7x, 256 devices: a whole 4x4x8 slice. The times are simulated.
256 devices in a mesh: ctx: 64 (over y, x, z_hi), ch: 2 (over core), fsdp: 2 (over z_lo).
Axes of the slice: x: 4, y: 4, z: 8 (z_hi: 4, z_lo: 2; z = z_hi * 2 + z_lo), core: 2. Of those that a mesh axis runs over, the one named last changes fastest.
Arguments:
- query_rows: bfloat16 [16384, 8192], P(('ctx', 'fsdp'), 'ch'), may hold values from -6 to 6
- key_rows: bfloat16 [16384, 8192], P(('ctx', 'fsdp'), 'ch'), may hold values from -6 to 6
- value_rows: bfloat16 [16384, 8192], P(('ctx', 'fsdp'), 'ch'), may hold values from -6 to 6
- upstream: bfloat16 [16384, 8192], P(('ctx', 'fsdp'), 'ch'), may hold values from -6 to 6
- decay_rate: float32 [8, 512], P(None, 'fsdp'), may hold values from 0.1 to 341
- residue: float32 [8, 512], P(None, 'fsdp'), may hold values from -4 to 4
Outputs:
- grad_query: bfloat16 [16384, 8192], P(('ctx', 'fsdp'), 'ch')
- grad_key: bfloat16 [16384, 8192], P(('ctx', 'fsdp'), 'ch')
- grad_value: bfloat16 [16384, 8192], P(('ctx', 'fsdp'), 'ch')
- residue_grad: float32 [8, 512], P(None, 'fsdp')
All inputs are finite; a program needn't handle non-finite values.
Results may differ from a plain program's by a relative error of at most 0.0017.
Values sent between devices are 32-bit elements; how exact they have to be, the bound alone decides.
No kernel may reach another device: no remote copies, remote signals or barrier semaphores. Data moves between devices by JAX's collectives and lax.ppermute only.
A program may use at most 128 MiB of HBM per device.

v0:
```python
import math
import jax
import jax.numpy as jnp
from jax import lax
from jax.sharding import PartitionSpec as P


def carried_in(part, axis, combine, identity, reverse):
    count = lax.axis_size(axis)
    place = lax.axis_index(axis)
    ahead = count - 1 - place if reverse else place
    gathered = jax.tree.map(lambda a: lax.all_gather(a, axis), part)
    state = jax.tree.map(lambda a, e: jnp.zeros_like(a) + jnp.asarray(e, a.dtype), part, identity)

    def one(lap, state):
        source = count - 1 - lap if reverse else lap
        return combine(
            state, jax.tree.map(lambda a: lax.dynamic_index_in_dim(a, source, 0, False), gathered)
        )

    return lax.fori_loop(0, ahead, one, state)


def to_blocks(matrix, block_count, width):
    return matrix.reshape(matrix.shape[0], block_count, width).transpose(1, 0, 2)


def from_blocks(blocked):
    return blocked.transpose(1, 0, 2).reshape(blocked.shape[1], -1)


def local(query_rows, key_rows, value_rows, upstream, decay_rate, residue):
    rates, residues = (
        lax.all_gather(decay_rate, "fsdp", axis=1, tiled=True),
        lax.all_gather(residue, "fsdp", axis=1, tiled=True),
    )
    row_count = query_rows.shape[0]
    local_width = query_rows.shape[1]
    width = rates.shape[1]
    modes = rates.shape[0]
    block_count = local_width // width
    tokens = row_count * lax.axis_size("ctx") * lax.axis_size("fsdp")
    log_decay = rates / tokens
    mode_gain = jnp.sqrt((1.0 + rates) / tokens)
    weight = residues * mode_gain
    positions = jnp.arange(row_count, dtype=jnp.float32)[:, None, None]
    blocks = tuple(
        (
            to_blocks(matrix, block_count, width)
            for matrix in (query_rows, key_rows, value_rows, upstream)
        )
    )
    span = min(row_count, 128)
    steps_in = jnp.arange(span, dtype=jnp.float32)[:, None, None]
    rising = jnp.exp(log_decay * steps_in)
    falling = jnp.exp(-log_decay * steps_in)
    index_row = jnp.arange(span)[:, None]
    index_col = jnp.arange(span)[None, :]
    lower_ones = (index_row >= index_col).astype(jnp.float32)
    upper_ones = (index_row <= index_col).astype(jnp.float32)
    enter_next = jnp.exp(-log_decay * (steps_in + 1.0))
    enter_prior = jnp.exp(-log_decay * (span - steps_in))

    def summarize(block):
        query_part, key_part, value_part, grad_part = block
        product = key_part.astype(jnp.float32) * value_part.astype(jnp.float32)
        gated = grad_part.astype(jnp.float32) * query_part.astype(jnp.float32)
        tail = jnp.exp(-log_decay * (row_count - 1.0 - positions))
        head = jnp.exp(-log_decay * positions)
        return (
            jnp.sum(tail * product[:, None, :], axis=0),
            jnp.sum(head * gated[:, None, :], axis=0),
        )

    ahead, behind = lax.map(summarize, blocks)

    def combine(earlier, later):
        return (earlier[0] + later[0], later[1] + jnp.exp(-log_decay * later[0][0]) * earlier[1])

    identity = (jnp.zeros((1,), jnp.float32), jnp.zeros_like(ahead))
    single = jnp.full((1,), float(row_count), jnp.float32)
    carry_ahead = carried_in((single, ahead), ("ctx", "fsdp"), combine, identity, False)[1]
    carry_behind = carried_in((single, behind), ("ctx", "fsdp"), combine, identity, True)[1]

    def running(ones, scaled):
        flat = scaled.reshape(span, -1)
        summed = jnp.dot(
            ones, flat, precision=lax.Precision.HIGHEST, preferred_element_type=jnp.float32
        )
        return summed.reshape(span, modes, width)

    def finish(block):
        query_part, key_part, value_part, grad_part, enter_ahead, enter_behind = block
        product = key_part.astype(jnp.float32) * value_part.astype(jnp.float32)
        gated = grad_part.astype(jnp.float32) * query_part.astype(jnp.float32)
        state = enter_ahead
        terms = jnp.zeros((modes, width), jnp.float32)
        states = falling * running(lower_ones, rising * product[:, None, :]) + enter_next * state
        conv_parts = [jnp.sum(weight * states, axis=1)]
        terms = terms + jnp.sum(gated[:, None, :] * states, axis=0)
        state = enter_behind
        flow_parts = []
        states = rising * running(upper_ones, falling * gated[:, None, :]) + enter_prior * state
        flow_parts.insert(0, jnp.sum(weight * states, axis=1))
        conv = jnp.concatenate(conv_parts, axis=0)
        flowing = jnp.concatenate(flow_parts, axis=0)
        grad_q = (grad_part.astype(jnp.float32) * conv).astype(jnp.bfloat16)
        grad_k = (flowing * value_part.astype(jnp.float32)).astype(jnp.bfloat16)
        grad_v = (flowing * key_part.astype(jnp.float32)).astype(jnp.bfloat16)
        return (grad_q, grad_k, grad_v, terms)

    query_grads, key_grads, value_grads, all_terms = lax.map(
        finish, blocks + (carry_ahead, carry_behind)
    )
    partial_grad = mode_gain * jnp.sum(all_terms, axis=0) / math.sqrt(tokens)
    summed = lax.psum(partial_grad, ("ctx", "ch"))
    residue_grad = lax.psum_scatter(summed, "fsdp", scatter_dimension=1, tiled=True)
    return (
        from_blocks(query_grads),
        from_blocks(key_grads),
        from_blocks(value_grads),
        residue_grad,
    )


def solution(mesh):
    placed = (
        P(("ctx", "fsdp"), "ch"),
        P(("ctx", "fsdp"), "ch"),
        P(("ctx", "fsdp"), "ch"),
        P(("ctx", "fsdp"), "ch"),
        P(None, "fsdp"),
        P(None, "fsdp"),
    )
    return jax.shard_map(
        local,
        mesh=mesh,
        in_specs=placed,
        out_specs=(
            P(("ctx", "fsdp"), "ch"),
            P(("ctx", "fsdp"), "ch"),
            P(("ctx", "fsdp"), "ch"),
            P(None, "fsdp"),
        ),
        check_vma=False,
    )
```

profile of v0, /device:TPU:32, one launch (start us, length us, event | category | flops | bytes accessed | tf_op | source)
XLA Modules:
  0.0 1259.8 jit_solution(2737631735284426398)
XLA Ops:
  7.2 4.7 all_gather.23
  11.9 4.6 all_gather.22
  16.5 1.7 copy.34
  20.2 1.6 copy.33
  23.8 36.9 %while.64 = (s32[]{:T(128)}, f32[8,8,512]{2,1,0:T(8,128)}, f32[8,8,512]{2,1,0:T(8,128)}, f32[1,8,512]{2,1,0:T(8,128)}, bf16[8,128,512]{1,2,0:T(8,128)(2,1)S(1)},...) while((s32[]{:T(128)}, f32[8,8,512]{2,1,0:T(8,128)}, ...), condition=%wide.region_3.4_spmd.clone.clone, body=%wide.region_0.3_spmd.clone.clone.sunk | while | flops 3530882 | bytes 3786349 | solution.py:75
  26.0 1.7 fusion.52
  30.7 1.7 fusion.52
  35.3 1.7 fusion.52
  39.9 1.7 fusion.52
  44.5 1.7 fusion.52
  49.1 1.7 fusion.52
  53.7 1.7 fusion.52
  58.3 1.7 fusion.52
  63.5 350.4 %all-reduce = f32[128]{0:T(128)S(1)} all-reduce(f32[128]{0:T(128)S(1)} %dynamic-update-slice), channel_id=1, replica_groups=mesh['ctx'=64,'ch'=2,'fsdp'=2] {'ctx','fsdp'}, use_global_device_ids=true, to_apply=%add | all-reduce | flops 128 | bytes 1024
  414.0 372.6 %while.63 = (s32[]{:T(128)}, f32[8,8,512]{2,1,0:T(8,128)S(1)}, s32[]{:T(128)}, f32[128,8,8,512]{3,2,1,0:T(8,128)}, f32[128,1]{0,1:T(1,128)S(1)}, /*index=5*/f32[...) while((s32[]{:T(128)}, f32[8,8,512]{2,1,0:T(8,128)S(1)}, s32[]{:T(128)}, ...), condition=%wide.region_7.8_spmd, body=%wide.region_6.7_spmd.sunk | while | flops 69638 | bytes 442535 | solution.py:21
  414.6 1.4 exponential_bitcast_fusion.5
  417.6 1.4 exponential_bitcast_fusion.5
  420.5 1.4 exponential_bitcast_fusion.5
  423.5 1.4 exponential_bitcast_fusion.5
  426.4 1.4 exponential_bitcast_fusion.5
  429.4 1.4 exponential_bitcast_fusion.5
  432.3 1.4 exponential_bitcast_fusion.5
  435.3 1.4 exponential_bitcast_fusion.5
  438.3 1.4 exponential_bitcast_fusion.5
  441.2 1.4 exponential_bitcast_fusion.5
  444.2 1.4 exponential_bitcast_fusion.5
  447.1 1.4 exponential_bitcast_fusion.5
  450.1 1.4 exponential_bitcast_fusion.5
  453.0 1.4 exponential_bitcast_fusion.5
  479.7 1.4 exponential_bitcast_fusion.5
  535.8 1.4 exponential_bitcast_fusion.5
  592.0 1.4 exponential_bitcast_fusion.5
  648.2 1.4 exponential_bitcast_fusion.5
  704.4 1.4 exponential_bitcast_fusion.5
  760.6 1.4 exponential_bitcast_fusion.5
  786.6 2.9 while.62
  790.2 94.5 %while.65 = (s32[]{:T(128)}, bf16[8,128,512]{1,2,0:T(8,128)(2,1)}, bf16[8,128,512]{1,2,0:T(8,128)(2,1)}, bf16[8,128,512]{1,2,0:T(8,128)(2,1)}, f32[8,8,512]{2,1,...) while((s32[]{:T(128)}, bf16[8,128,512]{1,2,0:T(8,128)(2,1)}, ...), condition=%wide.region_12.13_spmd.clone.clone, body=%wide.region_8.12_spmd.clone.clone.sunk | while | flops 1624109056 | bytes 28904616 | solution.py:112
  792.4 2.3 fusion.58
  794.7 1.8 fusion.59
  796.5 3.4 fusion.60
  804.3 2.3 fusion.58
  806.5 1.8 fusion.59
  808.4 3.4 fusion.60
  816.1 2.3 fusion.58
  818.3 1.8 fusion.59
  820.2 3.4 fusion.60
  827.9 2.3 fusion.58
  830.1 1.8 fusion.59
  832.0 3.4 fusion.60
  839.7 2.3 fusion.58
  842.0 1.8 fusion.59
  843.8 3.4 fusion.60
  851.5 2.2 fusion.58
  853.7 1.8 fusion.59
  855.6 3.4 fusion.60
  863.3 2.3 fusion.58
  865.6 1.8 fusion.59
  867.4 3.4 fusion.60
  875.1 2.3 fusion.58
  877.4 1.8 fusion.59
  879.2 3.4 fusion.60
  886.4 2.4 copy.43
  891.3 6.6 reduce-scatter.2.cloned.1.call-done
  898.0 355.3 %psum.8 = f32[8,256]{1,0:T(8,128)} all-reduce(f32[8,256]{1,0:T(8,128)} %reduce-scatter.2.cloned.1.call-done), channel_id=1, replica_groups=mesh['ctx'=64,'ch'=2,'fsdp'=2] {'ctx','ch'}, use_global_device_ids=true, to_apply=%region_14.15 | all-reduce | flops 2048 | bytes 16384 | tf_op jit(solution)/shard_map/psum | solution.py:116
  (580 shorter events, 413.0 us)
Async XLA Ops:
  7.2 11.0 copy-start.1
  7.2 406.7 %all-gather.7.cloned.1.call-start = ((), (), s32[]{:S(2)}) async-start(), calls=%async_computation.2 | async-start | bytes 16908288 | tf_op jit(solution)/shard_map/all_gather | solution.py:12
  11.9 9.9 copy-start.6
  16.5 3.0 copy-start.2
  60.7 725.8 %all-gather.5.cloned.1.call-start = ((), (), s32[]{:S(2)}) async-start(), calls=%async_computation.1 | async-start | bytes 16908288 | tf_op jit(solution)/shard_map/all_gather | solution.py:12
  61.5 836.5 %reduce-scatter.2.cloned.1.call-start = ((), (), s32[]{:S(2)}) async-start(), calls=%async_computation.3 | async-start | bytes 24576 | tf_op jit(solution)/shard_map/reduce_scatter | solution.py:117
  413.9 376.2 %copy-start = (f32[8,512]{1,0:T(8,128)S(1)}, f32[8,512]{1,0:T(8,128)}, u32[]{:S(2)}) copy-start(f32[8,512]{1,0:T(8,128)} %get-tuple-element.1009) | copy-start | bytes 49156
  414.0 376.2 %copy-start.5 = (f32[8,512]{1,0:T(8,128)S(1)}, f32[8,512]{1,0:T(8,128)}, u32[]{:S(2)}) copy-start(f32[8,512]{1,0:T(8,128)} %get-tuple-element.1003) | copy-start | bytes 49156
  790.2 95.5 %copy-start.7 = (f32[8,512]{1,0:T(8,128)S(1)}, f32[8,512]{1,0:T(8,128)}, u32[]{:S(2)}) copy-start(f32[8,512]{1,0:T(8,128)} %copy-done.6) | copy-start | bytes 49156
  884.7 4.0 copy-start.3
  886.4 3.7 copy-start.4
Sparse Core Ops, SparseCore 0:
  60.8 151.9 all-gather.6
  216.5 147.9 all-gather.4
  886.5 11.4 reduce-scatter.1
where the time goes:
time: 1270 us; the launch traced here: 1260 us
  blocking collectives  715 us (56%)
  other arithmetic  373 us (29%)
  local copies, waits for them, and re-layouts  113 us (9%)
  matrix products  32.6 us (3%)
  between operations  13.9 us (1%)
    psum x1, blocking collectives, local(): summed = lax.psum(partial_grad, ('ctx', 'ch'))  355 us
    unnamed x1, blocking collectives  350 us
    exp x127, other arithmetic, combine(): jnp.exp(-log_decay * later[0][0]) * earlier[1]  172 us
    add x127, other arithmetic, combine(): later[1] + jnp.exp(-log_decay * later[0][0]) * earlier[1]  122 us
    dynamic_slice x127, local copies, waits for them, and re-layouts, one(): lax.dynamic_index_in_dim(a, source, 0, False)  77.7 us
    dot_general x16, matrix products, running(): jnp.dot(ones, flat, precision=lax.Precision.HIGHEST, preferred_element_ty...  32.6 us
    reduce_sum x8, other arithmetic, finish(): flow_parts.insert(0, jnp.sum(weight * states, axis=1))  27.3 us
  transfers between devices with their start and end apart: 3, of which 1 were waited for; matrix products, arithmetic and copies ran while one was open for 30% of the time, Pallas kernels for 0%

commit v1 on v0

--- a/solution.py
+++ b/solution.py
@@ -113,7 +113,7 @@
         finish, blocks + (carry_ahead, carry_behind)
     )
     partial_grad = mode_gain * jnp.sum(all_terms, axis=0) / math.sqrt(tokens)
-    summed = lax.psum(partial_grad, ("ctx", "ch"))
+    summed = lax.psum(lax.psum(partial_grad, "ch"), "ctx")
     residue_grad = lax.psum_scatter(summed, "fsdp", scatter_dimension=1, tiled=True)
     return (
         from_blocks(query_grads),

time: 1270 us -> 1120 us (0.88)
  blocking collectives: 715 us -> 559 us
    psum x1 -> x2, blocking collectives: 355 us -> 199 us  [local(): summed = lax.psum(lax.psum(partial_grad, 'ch'), 'ctx')]
  transfers between devices with their start and end apart: 3 -> 3, of which waited for: 1 -> 1; matrix products, arithmetic and copies ran while one was open for 30% -> 34% of each run, Pallas kernels for 0% -> 0%
where the time goes in v1:
time: 1120 us; the launch traced here: 1100 us
  blocking collectives  559 us (50%)
  other arithmetic  370 us (33%)
  local copies, waits for them, and re-layouts  114 us (10%)
  matrix products  32.5 us (3%)
  between operations  13.9 us (1%)
    unnamed x1, blocking collectives  350 us
    psum x2, blocking collectives, local(): summed = lax.psum(lax.psum(partial_grad, 'ch'), 'ctx')  199 us
    exp x127, other arithmetic, combine(): jnp.exp(-log_decay * later[0][0]) * earlier[1]  169 us
    add x127, other arithmetic, combine(): later[1] + jnp.exp(-log_decay * later[0][0]) * earlier[1]  122 us
    dynamic_slice x127, local copies, waits for them, and re-layouts, one(): lax.dynamic_index_in_dim(a, source, 0, False)  78.3 us
    dot_general x16, matrix products, running(): jnp.dot(ones, flat, precision=lax.Precision.HIGHEST, preferred_element_ty...  32.5 us
    reduce_sum x8, other arithmetic, finish(): flow_parts.insert(0, jnp.sum(weight * states, axis=1))  27.3 us
  transfers between devices with their start and end apart: 3, of which 1 were waited for; matrix products, arithmetic and copies ran while one was open for 34% of the time, Pallas kernels for 0%

profile of v1, /device:TPU:32, one launch (start us, length us, event | category | flops | bytes accessed | tf_op | source)
XLA Modules:
  0.0 1103.2 jit_solution(15633426720602658693)
XLA Ops:
  7.2 4.7 all_gather.23
  11.9 4.6 all_gather.22
  16.5 1.7 copy.34
  20.2 1.6 copy.33
  23.8 36.9 %while.64 = (s32[]{:T(128)}, f32[8,8,512]{2,1,0:T(8,128)}, f32[8,8,512]{2,1,0:T(8,128)}, f32[1,8,512]{2,1,0:T(8,128)}, bf16[8,128,512]{1,2,0:T(8,128)(2,1)S(1)},...) while((s32[]{:T(128)}, f32[8,8,512]{2,1,0:T(8,128)}, ...), condition=%wide.region_3.4_spmd.clone.clone, body=%wide.region_0.3_spmd.clone.clone.sunk | while | flops 3530882 | bytes 3786349 | solution.py:75
  26.0 1.7 fusion.52
  30.6 1.7 fusion.52
  35.2 1.7 fusion.52
  39.8 1.7 fusion.52
  44.5 1.7 fusion.52
  49.1 1.7 fusion.52
  53.7 1.7 fusion.52
  58.3 1.7 fusion.52
  63.6 350.3 %all-reduce = f32[128]{0:T(128)S(1)} all-reduce(f32[128]{0:T(128)S(1)} %dynamic-update-slice), channel_id=1, replica_groups=mesh['ctx'=64,'ch'=2,'fsdp'=2] {'ctx','fsdp'}, use_global_device_ids=true, to_apply=%add | all-reduce | flops 128 | bytes 1024
  414.0 369.8 %while.63 = (s32[]{:T(128)}, f32[8,8,512]{2,1,0:T(8,128)S(1)}, s32[]{:T(128)}, f32[128,8,8,512]{3,2,1,0:T(8,128)}, f32[128,1]{0,1:T(1,128)S(1)}, /*index=5*/f32[...) while((s32[]{:T(128)}, f32[8,8,512]{2,1,0:T(8,128)S(1)}, s32[]{:T(128)}, ...), condition=%wide.region_7.8_spmd, body=%wide.region_6.7_spmd.sunk | while | flops 69638 | bytes 442535 | solution.py:21
  414.6 1.3 exponential_bitcast_fusion.5
  417.5 1.3 exponential_bitcast_fusion.5
  435.1 1.3 exponential_bitcast_fusion.5
  452.8 1.3 exponential_bitcast_fusion.5
  455.7 1.3 exponential_bitcast_fusion.5
  470.4 1.3 exponential_bitcast_fusion.5
  473.3 1.3 exponential_bitcast_fusion.5
  490.9 1.3 exponential_bitcast_fusion.5
  508.5 1.3 exponential_bitcast_fusion.5
  511.5 1.3 exponential_bitcast_fusion.5
  526.1 1.3 exponential_bitcast_fusion.5
  529.1 1.3 exponential_bitcast_fusion.5
  546.7 1.3 exponential_bitcast_fusion.5
  564.3 1.3 exponential_bitcast_fusion.5
  567.2 1.3 exponential_bitcast_fusion.5
  581.9 1.3 exponential_bitcast_fusion.5
  584.8 1.3 exponential_bitcast_fusion.5
  602.5 1.3 exponential_bitcast_fusion.5
  783.9 3.0 while.62
  784.5 1.4 exponential_bitcast_fusion.4
  787.5 94.5 %while.65 = (s32[]{:T(128)}, bf16[8,128,512]{1,2,0:T(8,128)(2,1)}, bf16[8,128,512]{1,2,0:T(8,128)(2,1)}, bf16[8,128,512]{1,2,0:T(8,128)(2,1)}, f32[8,8,512]{2,1,...) while((s32[]{:T(128)}, bf16[8,128,512]{1,2,0:T(8,128)(2,1)}, ...), condition=%wide.region_12.13_spmd.clone.clone, body=%wide.region_8.12_spmd.clone.clone.sunk | while | flops 1624109056 | bytes 28904616 | solution.py:112
  789.7 2.3 fusion.58
  792.0 1.8 fusion.59
  793.8 3.4 fusion.60
  801.5 2.3 fusion.58
  803.8 1.8 fusion.59
  805.6 3.4 fusion.60
  813.3 2.3 fusion.58
  815.6 1.8 fusion.59
  817.4 3.4 fusion.60
  825.1 2.3 fusion.58
  827.4 1.8 fusion.59
  829.2 3.4 fusion.60
  837.0 2.3 fusion.58
  839.2 1.8 fusion.59
  841.1 3.4 fusion.60
  848.8 2.3 fusion.58
  851.0 1.8 fusion.59
  852.9 3.4 fusion.60
  860.6 2.2 fusion.58
  862.8 1.8 fusion.59
  864.7 3.4 fusion.60
  872.4 2.2 fusion.58
  874.6 1.8 fusion.59
  876.5 3.4 fusion.60
  883.6 2.4 copy.43
  888.6 8.6 reduce-scatter.2.cloned.1.call-done
  897.2 2.6 psum.17
  899.8 196.9 %psum.16 = f32[8,256]{1,0:T(8,128)} all-reduce(f32[8,256]{1,0:T(8,128)S(1)} %psum.17), channel_id=1, replica_groups=mesh['ctx'=64,'ch'=2,'fsdp'=2] {'ctx'}, use_global_device_ids=true, to_apply=%region_15.16 | all-reduce | flops 2048 | bytes 16384 | tf_op jit(solution)/shard_map/psum | solution.py:116
  (581 shorter events, 412.2 us)
Async XLA Ops:
  7.2 11.0 %copy-start.1 = (bf16[128,4096]{1,0:T(8,128)(2,1)S(1)}, bf16[128,4096]{1,0:T(8,128)(2,1)}, u32[]{:S(2)}) copy-start(bf16[128,4096]{1,0:T(8,128)(2,1)} %param.14) | copy-start | bytes 3145732
  7.2 406.7 %all-gather.7.cloned.1.call-start = ((), (), s32[]{:S(2)}) async-start(), calls=%async_computation.2 | async-start | bytes 16908288 | tf_op jit(solution)/shard_map/all_gather | solution.py:12
  11.9 9.9 copy-start.6
  16.5 3.0 copy-start.2
  60.7 723.2 %all-gather.5.cloned.1.call-start = ((), (), s32[]{:S(2)}) async-start(), calls=%async_computation.1 | async-start | bytes 16908288 | tf_op jit(solution)/shard_map/all_gather | solution.py:12
  61.4 835.8 %reduce-scatter.2.cloned.1.call-start = ((), (), s32[]{:S(2)}) async-start(), calls=%async_computation.3 | async-start | bytes 24576 | tf_op jit(solution)/shard_map/reduce_scatter | solution.py:117
  413.9 373.5 %copy-start = (f32[8,512]{1,0:T(8,128)S(1)}, f32[8,512]{1,0:T(8,128)}, u32[]{:S(2)}) copy-start(f32[8,512]{1,0:T(8,128)} %get-tuple-element.1009) | copy-start | bytes 49156
  413.9 373.5 %copy-start.5 = (f32[8,512]{1,0:T(8,128)S(1)}, f32[8,512]{1,0:T(8,128)}, u32[]{:S(2)}) copy-start(f32[8,512]{1,0:T(8,128)} %get-tuple-element.1003) | copy-start | bytes 49156
  787.5 95.5 %copy-start.7 = (f32[8,512]{1,0:T(8,128)S(1)}, f32[8,512]{1,0:T(8,128)}, u32[]{:S(2)}) copy-start(f32[8,512]{1,0:T(8,128)} %copy-done.6) | copy-start | bytes 49156
  882.0 4.0 copy-start.3
  883.6 3.7 copy-start.4
Sparse Core Ops, SparseCore 0:
  60.8 151.7 all-gather.6
  216.3 147.9 all-gather.4
  883.7 13.4 reduce-scatter.1
